TPU v7x, 32 devices: a whole 2x2x4 slice. The times are simulated.
32 devices in a mesh: head: 4 (over y, x), ctx: 8 (over z, core).
Axes of the slice: x: 2, y: 2, z: 4, core: 2. Of those that a mesh axis runs over, the one named last changes fastest.
Arguments:
- query_in: bfloat16 [4096, 4096], P(('ctx', 'head')), may hold values from -6 to 6
- key_in: bfloat16 [4096, 1024], P(('ctx', 'head')), may hold values from -6 to 6
- value_in: bfloat16 [4096, 1024], P(('ctx', 'head')), may hold values from -6 to 6
- attn_out: bfloat16 [4096, 4096], P(('ctx', 'head')), may hold values from -2 to 2
- out_grad: bfloat16 [4096, 4096], P(('ctx', 'head')), may hold values from -6 to 6
- log_norm: float32 [4096, 32], P(('ctx', 'head')), may hold values from 4 to 8
- doc_ids: int32 [4096], replicated, may hold values from 0 to 15, never falling along the last dimension, each value on 1 to 512 neighbouring positions
Outputs:
- query_grad: bfloat16 [4096, 4096], P(('ctx', 'head'))
- key_grad: bfloat16 [4096, 1024], P(('ctx', 'head'))
- value_grad: bfloat16 [4096, 1024], P(('ctx', 'head'))
Inputs may be any that keep to these rules, and one draw needn't show every extreme that they name: `doc_ids`: document numbers never fall along the sequence and start at 0; every document has 1 to 512 tokens and one has exactly 512.
All inputs are finite; a program needn't handle non-finite values.
Results may differ from a plain program's by a relative error of at most 0.0049.
Values may be sent and summed in bfloat16 or wider, within the bound.
No kernel may reach another device: no remote copies, remote signals or barrier semaphores. Data moves between devices by JAX's collectives and lax.ppermute only.
A program may use at most 128 MiB of HBM per device.

v0:
```python
import jax
import jax.numpy as jnp
from jax import lax
from jax.sharding import PartitionSpec as P

HEAD_DIM = 128


def shifted(value, axis, by):
    count = lax.axis_size(axis)
    pairs = [(i, i + by) for i in range(count) if 0 <= i + by < count]
    return lax.ppermute(value, axis, pairs)


def shifted_2(value, axis, by):
    count = lax.axis_size(axis)
    return lax.ppermute(value, axis, [(i, (i + by) % count) for i in range(count)])


def block_terms(
    query_rows,
    dout_rows,
    norm_rows,
    delta_rows,
    query_ids,
    query_start,
    key_rows,
    value_rows,
    key_ids,
    key_start,
):
    r = query_rows.shape[0]
    c = key_rows.shape[0]
    kv_local = key_rows.shape[1] // HEAD_DIM
    heads_local = query_rows.shape[1] // HEAD_DIM
    group = heads_local // kv_local
    scaling = HEAD_DIM ** (-0.5)
    query_heads = query_rows.reshape(r, kv_local, group, HEAD_DIM)
    dout_heads = dout_rows.reshape(r, kv_local, group, HEAD_DIM)
    key_heads = key_rows.reshape(c, kv_local, HEAD_DIM)
    value_heads = value_rows.reshape(c, kv_local, HEAD_DIM)
    scores = (
        jnp.einsum("qgjd,kgd->gjqk", query_heads, key_heads, preferred_element_type=jnp.float32)
        * scaling
    )
    norm_cols = jnp.transpose(norm_rows.reshape(r, kv_local, group), (1, 2, 0))[..., None]
    delta_cols = jnp.transpose(delta_rows.reshape(r, kv_local, group), (1, 2, 0))[..., None]
    query_pos = query_start + jnp.arange(r, dtype=jnp.int32)
    key_pos = key_start + jnp.arange(c, dtype=jnp.int32)
    allowed = (query_ids[:, None] == key_ids[None, :]) & (query_pos[:, None] >= key_pos[None, :])
    weights = jnp.where(allowed, jnp.exp(scores - norm_cols), 0.0)
    weights_low = weights.astype(jnp.bfloat16)
    grad_value = jnp.einsum(
        "gjqk,qgjd->kgd", weights_low, dout_heads, preferred_element_type=jnp.float32
    )
    prob_grad = jnp.einsum(
        "qgjd,kgd->gjqk", dout_heads, value_heads, preferred_element_type=jnp.float32
    )
    score_grad = (weights * (prob_grad - delta_cols)).astype(jnp.bfloat16)
    grad_query = (
        jnp.einsum("gjqk,kgd->qgjd", score_grad, key_heads, preferred_element_type=jnp.float32)
        * scaling
    )
    grad_key = (
        jnp.einsum("gjqk,qgjd->kgd", score_grad, query_heads, preferred_element_type=jnp.float32)
        * scaling
    )
    return (
        grad_query.reshape(r, heads_local * HEAD_DIM),
        grad_key.reshape(c, kv_local * HEAD_DIM),
        grad_value.reshape(c, kv_local * HEAD_DIM),
    )


def head_delta(dout_rows, output_rows):
    row_count = dout_rows.shape[0]
    product = dout_rows.astype(jnp.float32) * output_rows.astype(jnp.float32)
    return jnp.sum(product.reshape(row_count, -1, HEAD_DIM), axis=2)


def local(query_in, key_in, value_in, attn_out, out_grad, log_norm, doc_ids):
    query_rows, key_rows, value_rows, dout_rows, output_rows = (
        lax.all_to_all(query_in, "head", split_axis=1, concat_axis=0, tiled=True),
        lax.all_to_all(key_in, "head", split_axis=1, concat_axis=0, tiled=True),
        lax.all_to_all(value_in, "head", split_axis=1, concat_axis=0, tiled=True),
        lax.all_to_all(attn_out, "head", split_axis=1, concat_axis=0, tiled=True),
        lax.all_to_all(out_grad, "head", split_axis=1, concat_axis=0, tiled=True),
    )
    norm_rows = lax.all_to_all(log_norm, "head", split_axis=1, concat_axis=0, tiled=True)
    dout_rows, output_rows = (output_rows, dout_rows)
    delta_rows = head_delta(dout_rows, output_rows)
    row_count = query_rows.shape[0]
    cycle_size = lax.axis_size("ctx")
    my_index = lax.axis_index("ctx")
    my_start = my_index * row_count
    visits = min(cycle_size, row_count // row_count + 1)

    def ids_at(start):
        return lax.dynamic_slice_in_dim(doc_ids, start, row_count)

    my_ids = ids_at(my_start)
    query_zero = jnp.zeros(query_rows.shape, jnp.float32)
    key_zero = jnp.zeros(key_rows.shape, jnp.float32)

    def skipped(_):
        return (query_zero, key_zero, key_zero)

    key_value = jnp.stack((key_rows, value_rows))

    def visit_block(held_pair, grad_pair, source):
        key_start = source * row_count

        def compute(_):
            return block_terms(
                query_rows,
                dout_rows,
                norm_rows,
                delta_rows,
                my_ids,
                my_start,
                held_pair[0],
                held_pair[1],
                ids_at(key_start),
                key_start,
            )

        grad_query, grad_key, grad_value = lax.cond(source <= my_index, compute, skipped, 0)
        return (grad_query, grad_pair + jnp.stack((grad_key, grad_value)))

    def cycle_turn(turn_index, carry):
        held_pair, grad_pair, query_total = carry
        following = shifted(held_pair, "ctx", 1)
        grad_query, grad_pair = visit_block(
            held_pair, grad_pair, (my_index - turn_index) % cycle_size
        )
        grad_pair = shifted_2(grad_pair, "ctx", 1)
        return (following, grad_pair, query_total + grad_query)

    start = (key_value, jnp.zeros(key_value.shape, jnp.float32), query_zero)
    held_pair, grad_pair, query_total = lax.fori_loop(0, visits - 1, cycle_turn, start)
    grad_query, grad_pair = visit_block(
        held_pair, grad_pair, (my_index - (visits - 1)) % cycle_size
    )
    grad_pair = shifted_2(grad_pair.astype(jnp.bfloat16), "ctx", 1 - visits).astype(grad_pair.dtype)
    query_total = query_total + grad_query
    key_total = grad_pair[0]
    value_total = grad_pair[1]
    query_grad, key_grad, value_grad = (
        lax.all_to_all(
            query_total.astype(jnp.bfloat16), "head", split_axis=0, concat_axis=1, tiled=True
        ),
        lax.all_to_all(
            key_total.astype(jnp.bfloat16), "head", split_axis=0, concat_axis=1, tiled=True
        ),
        lax.all_to_all(
            value_total.astype(jnp.bfloat16), "head", split_axis=0, concat_axis=1, tiled=True
        ),
    )
    return (query_grad, key_grad, value_grad)


def solution(mesh):
    in_specs = (
        P(("ctx", "head"), None),
        P(("ctx", "head"), None),
        P(("ctx", "head"), None),
        P(("ctx", "head"), None),
        P(("ctx", "head"), None),
        P(("ctx", "head"), None),
        P(),
    )
    out_specs = (P(("ctx", "head"), None), P(("ctx", "head"), None), P(("ctx", "head"), None))
    return jax.shard_map(local, mesh=mesh, in_specs=in_specs, out_specs=out_specs, check_vma=False)
```

profile of v0, /device:TPU:8, one launch (start us, length us, event | category | flops | bytes accessed | tf_op | source)
XLA Modules:
  0.0 171.9 jit_solution(2658840993720488320)
XLA Ops:
  2.5 3.7 %all-to-all-start = ((bf16[128,4,256]{0,2,1:T(8,128)(2,1)}), bf16[128,4,256]{0,2,1:T(8,128)(2,1)S(1)}, u32[]{:S(2)}, u32[]{:S(2)}) async-start(bf16[128,4,256]{0,2,1:T(8,128)(2,1)} %bitcast.44), calls=%async_computation | async-start | bytes 524288 | tf_op jit(solution)/shard_map/all_to_all | solution.py:84
  8.0 3.6 %all-to-all-done = bf16[128,4,256]{0,2,1:T(8,128)(2,1)S(1)} async-done(((bf16[128,4,256]{0,2,1:T(8,128)(2,1)}), bf16[128,4,256]{0,2,1:T(8,128)(2,1)S(1)}, u32[]{:S(2)}, u32[]{:S(2)}) %all-to-all-start) | async-done | bytes 262176 | tf_op jit(solution)/shard_map/all_to_all | solution.py:84
  11.6 3.4 %all-to-all-start.1 = ((bf16[128,4,256]{0,2,1:T(8,128)(2,1)}), bf16[128,4,256]{0,2,1:T(8,128)(2,1)S(1)}, u32[]{:S(2)}, u32[]{:S(2)}) async-start(bf16[128,4,256]{0,2,1:T(8,128)(2,1)} %bitcast.47), calls=%async_computation.1 | async-start | bytes 524288 | tf_op jit(solution)/shard_map/all_to_all | solution.py:85
  17.3 3.1 %all-to-all-done.1 = bf16[128,4,256]{0,2,1:T(8,128)(2,1)S(1)} async-done(((bf16[128,4,256]{0,2,1:T(8,128)(2,1)}), bf16[128,4,256]{0,2,1:T(8,128)(2,1)S(1)}, u32[]{:S(2)}, u32[]{:S(2)}) %all-to-all-start.1) | async-done | bytes 262176 | tf_op jit(solution)/shard_map/all_to_all | solution.py:85
  21.1 3.5 %all-to-all-start.5 = ((bf16[128,4,1024]{0,2,1:T(8,128)(2,1)}), bf16[128,4,1024]{0,2,1:T(8,128)(2,1)S(1)}, u32[]{:S(2)}, u32[]{:S(2)}) async-start(bf16[128,4,1024]{0,2,1:T(8,128)(2,1)} %bitcast.59), calls=%async_computation.5 | async-start | bytes 2097152 | tf_op jit(solution)/shard_map/all_to_all | solution.py:86
  26.9 9.0 %all-to-all-done.5 = bf16[128,4,1024]{0,2,1:T(8,128)(2,1)S(1)} async-done(((bf16[128,4,1024]{0,2,1:T(8,128)(2,1)}), bf16[128,4,1024]{0,2,1:T(8,128)(2,1)S(1)}, u32[]{:S(2)}, u32[]{:S(2)}) %all-to-all-start.5) | async-done | bytes 1048608 | tf_op jit(solution)/shard_map/all_to_all | solution.py:86
  35.9 3.5 %all-to-all-start.4 = ((bf16[128,4,1024]{0,2,1:T(8,128)(2,1)}), bf16[128,4,1024]{0,2,1:T(8,128)(2,1)S(1)}, u32[]{:S(2)}, u32[]{:S(2)}) async-start(bf16[128,4,1024]{0,2,1:T(8,128)(2,1)} %bitcast.56), calls=%async_computation.4 | async-start | bytes 2097152 | tf_op jit(solution)/shard_map/all_to_all | solution.py:87
  40.7 11.8 %all-to-all-done.4 = bf16[128,4,1024]{0,2,1:T(8,128)(2,1)S(1)} async-done(((bf16[128,4,1024]{0,2,1:T(8,128)(2,1)}), bf16[128,4,1024]{0,2,1:T(8,128)(2,1)S(1)}, u32[]{:S(2)}, u32[]{:S(2)}) %all-to-all-start.4) | async-done | bytes 1048608 | tf_op jit(solution)/shard_map/all_to_all | solution.py:87
  52.5 3.5 %all-to-all-start.2 = ((bf16[128,4,1024]{0,2,1:T(8,128)(2,1)}), bf16[128,4,1024]{0,2,1:T(8,128)(2,1)S(1)}, u32[]{:S(2)}, u32[]{:S(2)}) async-start(bf16[128,4,1024]{0,2,1:T(8,128)(2,1)} %bitcast.177), calls=%async_computation.2 | async-start | bytes 2097152 | tf_op jit(solution)/shard_map/all_to_all | solution.py:83
  62.4 6.7 %all-to-all-done.2 = bf16[128,4,1024]{0,2,1:T(8,128)(2,1)S(1)} async-done(((bf16[128,4,1024]{0,2,1:T(8,128)(2,1)}), bf16[128,4,1024]{0,2,1:T(8,128)(2,1)S(1)}, u32[]{:S(2)}, u32[]{:S(2)}) %all-to-all-start.2) | async-done | bytes 1048608 | tf_op jit(solution)/shard_map/all_to_all | solution.py:83
  69.2 3.3 %all-to-all-start.3 = ((f32[128,4,8]{0,2,1:T(8,128)}), f32[128,4,8]{0,2,1:T(8,128)S(1)}, u32[]{:S(2)}, u32[]{:S(2)}) async-start(f32[128,4,8]{0,2,1:T(8,128)} %bitcast.53), calls=%async_computation.3 | async-start | bytes 32768 | tf_op jit(solution)/shard_map/all_to_all | solution.py:89
  77.1 18.2 %conditional.2 = (f32[512,1024]{0,1:T(8,128)}, f32[1,512,256]{1,2,0:T(8,128)}, f32[1,512,256]{1,2,0:T(8,128)}) conditional(s32[]{:T(128)} %convert_element_type.49, () %tuple.34, (s32[512]{0:T(512)S(1)}, s32[]{:T(128)}, s32[4096]{0:T(1024)}, s32[]{:T(128)}, bf16[2,512,256]{2,1,0:T(8,128)(2,1)}, /*index=5*/bf16[512,1024]{1,0:T(8,128)(2,1)S(1)}, ...), branch_computations={%region_1.2_spmd, %region_2.3_spmd} | conditional | flops 2706768896 | bytes 60457152 | solution.py:127
  85.3 2.7 %fusion.5 = f32[2,512,128,1]{1,2,3,0:T(8,128)} fusion(bf16[512,2,4,128]{0,3,2,1:T(8,128)(2,1)S(1)} %bitcast.184, f32[2,512,512,4]{2,1,3,0:T(8,128)S(1)} %fusion.26, f32[2,4,512]{2,1,0:T(4,128)S(1)} %bitcast.198, pred[512,512]{0,1:T(8,128)(4,1)S(1)} %copy-done.7), kind=kOutput, calls=%fused_computation.7 | convolution fusion | flops 545259520 | bytes 10240000 | tf_op jit(solution)/shard_map/while/body/eval_jaxpr/cond/branch_1_fun/gjqk,qgjd->kgd/dot_general | solution.py:53
  88.0 3.0 %fusion.1 = bf16[2,4,512,512]{2,3,1,0:T(8,128)(2,1)S(1)} fusion(f32[2,512,512,4]{2,1,3,0:T(8,128)S(1)} %fusion.26, f32[2,4,512]{2,1,0:T(4,128)S(1)} %bitcast.196, f32[2,4,512]{2,1,0:T(4,128)S(1)} %bitcast.199, pred[512,512]{0,1:T(8,128)(4,1)S(1)} %copy-done.7, bf16[512,2,128,1]{0,2,3,1:T(8,128)(2,1)S(1)} %bitcast.192, bf16[512,2,4,128]{0,3,2,1:T(8,128)(2,1)S(1)} %bitcast.185), kind=kOutput, calls=%fused_computation.2 | convolution fusion | flops 549453824 | bytes 14188544 | tf_op jit(solution)/shard_map/while/body/eval_jaxpr/cond/branch_1_fun/qgjd,kgd->gjqk/dot_general | solution.py:56
  97.6 3.6 %collective-permute-start = (bf16[2,512,256]{2,1,0:T(8,128)(2,1)}, bf16[2,512,256]{2,1,0:T(8,128)(2,1)S(1)}, u32[]{:S(2)}, u32[]{:S(2)}) collective-permute-start(bf16[2,512,256]{2,1,0:T(8,128)(2,1)} %pad_maximum_fusion.1), channel_id=1, source_target_pairs={{0,1},{1,2},{2,3},{3,4},{4,5},{5,6},{6,7},{8,9},{9,10},{10,11},{11... | collective-permute-start | bytes 1572872 | tf_op jit(solution)/shard_map/while/body/eval_jaxpr/ppermute | solution.py:12
  101.2 16.4 %collective-permute-done = bf16[2,512,256]{2,1,0:T(8,128)(2,1)S(1)} collective-permute-done((bf16[2,512,256]{2,1,0:T(8,128)(2,1)}, bf16[2,512,256]{2,1,0:T(8,128)(2,1)S(1)}, u32[]{:S(2)}, u32[]{:S(2)}) %collective-permute-start) | collective-permute-done | bytes 524320 | tf_op jit(solution)/shard_map/while/body/eval_jaxpr/ppermute | solution.py:12
  117.7 14.9 %conditional.3 = (f32[512,1024]{0,1:T(8,128)}, f32[1,512,256]{1,2,0:T(8,128)}, f32[1,512,256]{1,2,0:T(8,128)S(1)}) conditional(s32[]{:T(128)} %convert_element_type.53, () %tuple.36, (s32[512]{0:T(512)S(1)}, s32[]{:T(128)}, s32[4096]{0:T(1024)}, s32[]{:T(128)}, bf16[2,512,256]{2,1,0:T(8,128)(2,1)S(1)}, /*index=5*/bf16[512,1024]{1,0:T(8,128)(2,1)S(1)}, ...), branch_computations={%region_3.4_spmd, %region_4.5_spmd} | conditional | flops 2706768896 | bytes 59408520 | solution.py:127
  125.2 3.0 %fusion.12 = bf16[2,4,512,512]{2,3,1,0:T(8,128)(2,1)S(1)} fusion(f32[2,512,512,4]{2,1,3,0:T(8,128)S(1)} %fusion.27, f32[2,4,512]{2,1,0:T(4,128)S(1)} %bitcast.197, f32[2,4,512]{2,1,0:T(4,128)S(1)} %bitcast.201, pred[512,512]{0,1:T(8,128)(4,1)S(1)} %compare_and_fusion.1, bf16[512,2,128,1]{0,2,3,1:T(8,128)(2,1)S(1)} %bitcast.193, ...), kind=kOutput, calls=%fused_computation.19 | convolution fusion | flops 549453824 | bytes 14188544 | tf_op jit(solution)/shard_map/cond/branch_1_fun/qgjd,kgd->gjqk/dot_general | solution.py:56
  136.4 3.7 %all-to-all-start.6 = ((bf16[4,128,1024]{2,1,0:T(8,128)(2,1)}), bf16[4,128,1024]{2,1,0:T(8,128)(2,1)S(1)}, u32[]{:S(2)}, u32[]{:S(2)}) async-start(bf16[4,128,1024]{2,1,0:T(8,128)(2,1)} %bitcast.64), calls=%async_computation.6 | async-start | bytes 2097152 | tf_op jit(solution)/shard_map/all_to_all | solution.py:149
  141.8 6.7 %collective-permute-done.2 = bf16[2,512,256]{1,2,0:T(8,128)(2,1)S(1)} collective-permute-done((bf16[2,512,256]{1,2,0:T(8,128)(2,1)S(1)}, bf16[2,512,256]{1,2,0:T(8,128)(2,1)S(1)}, u32[]{:S(2)}, u32[]{:S(2)}) %collective-permute-start.2) | collective-permute-done | bytes 524320 | tf_op jit(solution)/shard_map/ppermute | solution.py:17
  149.3 4.0 %all-to-all-done.6 = bf16[4,128,1024]{2,1,0:T(8,128)(2,1)S(1)} async-done(((bf16[4,128,1024]{2,1,0:T(8,128)(2,1)}), bf16[4,128,1024]{2,1,0:T(8,128)(2,1)S(1)}, u32[]{:S(2)}, u32[]{:S(2)}) %all-to-all-start.6) | async-done | bytes 1048608 | tf_op jit(solution)/shard_map/all_to_all | solution.py:149
  153.3 3.4 %all-to-all-start.8 = ((bf16[4,128,256]{2,1,0:T(8,128)(2,1)}), bf16[4,128,256]{2,1,0:T(8,128)(2,1)S(1)}, u32[]{:S(2)}, u32[]{:S(2)}) async-start(bf16[4,128,256]{2,1,0:T(8,128)(2,1)} %bitcast.70), calls=%async_computation.8 | async-start | bytes 524288 | tf_op jit(solution)/shard_map/all_to_all | solution.py:155
  157.6 4.5 %all-to-all-done.8 = bf16[4,128,256]{2,1,0:T(8,128)(2,1)S(1)} async-done(((bf16[4,128,256]{2,1,0:T(8,128)(2,1)}), bf16[4,128,256]{2,1,0:T(8,128)(2,1)S(1)}, u32[]{:S(2)}, u32[]{:S(2)}) %all-to-all-start.8) | async-done | bytes 262176 | tf_op jit(solution)/shard_map/all_to_all | solution.py:155
  162.1 3.4 %all-to-all-start.7 = ((bf16[4,128,256]{2,1,0:T(8,128)(2,1)}), bf16[4,128,256]{2,1,0:T(8,128)(2,1)S(1)}, u32[]{:S(2)}, u32[]{:S(2)}) async-start(bf16[4,128,256]{2,1,0:T(8,128)(2,1)} %bitcast.67), calls=%async_computation.7 | async-start | bytes 524288 | tf_op jit(solution)/shard_map/all_to_all | solution.py:152
  (78 shorter events, 61.4 us)
Async XLA Ops:
  0.6 38.8 %copy-start.2 = (bf16[128,4096]{1,0:T(8,128)(2,1)S(1)}, bf16[128,4096]{1,0:T(8,128)(2,1)}, u32[]{:S(2)}) copy-start(bf16[128,4096]{1,0:T(8,128)(2,1)} %param.11) | copy-start | bytes 3145732
  2.5 9.1 %all-to-all-start = ((bf16[128,4,256]{0,2,1:T(8,128)(2,1)}), bf16[128,4,256]{0,2,1:T(8,128)(2,1)S(1)}, u32[]{:S(2)}, u32[]{:S(2)}) async-start(bf16[128,4,256]{0,2,1:T(8,128)(2,1)} %bitcast.44), calls=%async_computation | async-start | bytes 524288 | tf_op jit(solution)/shard_map/all_to_all | solution.py:84
  11.6 8.8 %all-to-all-start.1 = ((bf16[128,4,256]{0,2,1:T(8,128)(2,1)}), bf16[128,4,256]{0,2,1:T(8,128)(2,1)S(1)}, u32[]{:S(2)}, u32[]{:S(2)}) async-start(bf16[128,4,256]{0,2,1:T(8,128)(2,1)} %bitcast.47), calls=%async_computation.1 | async-start | bytes 524288 | tf_op jit(solution)/shard_map/all_to_all | solution.py:85
  20.4 0.7 copy-start.5
  21.1 14.8 %all-to-all-start.5 = ((bf16[128,4,1024]{0,2,1:T(8,128)(2,1)}), bf16[128,4,1024]{0,2,1:T(8,128)(2,1)S(1)}, u32[]{:S(2)}, u32[]{:S(2)}) async-start(bf16[128,4,1024]{0,2,1:T(8,128)(2,1)} %bitcast.59), calls=%async_computation.5 | async-start | bytes 2097152 | tf_op jit(solution)/shard_map/all_to_all | solution.py:86
  35.9 16.6 %all-to-all-start.4 = ((bf16[128,4,1024]{0,2,1:T(8,128)(2,1)}), bf16[128,4,1024]{0,2,1:T(8,128)(2,1)S(1)}, u32[]{:S(2)}, u32[]{:S(2)}) async-start(bf16[128,4,1024]{0,2,1:T(8,128)(2,1)} %bitcast.56), calls=%async_computation.4 | async-start | bytes 2097152 | tf_op jit(solution)/shard_map/all_to_all | solution.py:87
  52.5 16.6 %all-to-all-start.2 = ((bf16[128,4,1024]{0,2,1:T(8,128)(2,1)}), bf16[128,4,1024]{0,2,1:T(8,128)(2,1)S(1)}, u32[]{:S(2)}, u32[]{:S(2)}) async-start(bf16[128,4,1024]{0,2,1:T(8,128)(2,1)} %bitcast.177), calls=%async_computation.2 | async-start | bytes 2097152 | tf_op jit(solution)/shard_map/all_to_all | solution.py:83
  69.2 4.9 %copy-start = (bf16[128,4,1024]{0,2,1:T(8,128)(2,1)}, bf16[128,4,1024]{0,2,1:T(8,128)(2,1)S(1)}, u32[]{:S(2)}) copy-start(bf16[128,4,1024]{0,2,1:T(8,128)(2,1)S(1)} %all-to-all-done.2) | copy-start | bytes 3145732
  69.2 7.9 %all-to-all-start.3 = ((f32[128,4,8]{0,2,1:T(8,128)}), f32[128,4,8]{0,2,1:T(8,128)S(1)}, u32[]{:S(2)}, u32[]{:S(2)}) async-start(f32[128,4,8]{0,2,1:T(8,128)} %bitcast.53), calls=%async_computation.3 | async-start | bytes 32768 | tf_op jit(solution)/shard_map/all_to_all | solution.py:89
  82.9 2.4 %copy-start.3 = (bf16[512,1024]{0,1:T(8,128)(2,1)S(1)}, bf16[512,1024]{0,1:T(8,128)(2,1)}, u32[]{:S(2)}) copy-start(bf16[512,1024]{0,1:T(8,128)(2,1)} %copy.139) | copy-start | bytes 3145732 | tf_op jit(solution)/shard_map/while/body/eval_jaxpr/cond
  82.9 2.4 %copy-start.7 = (pred[512,512]{0,1:T(8,128)(4,1)S(1)}, pred[512,512]{0,1:T(8,128)(4,1)}, u32[]{:S(2)}) copy-start(pred[512,512]{0,1:T(8,128)(4,1)} %compare_and_fusion) | copy-start | bytes 786436 | tf_op jit(solution)/shard_map/while/body/eval_jaxpr/cond
  85.3 2.7 %copy-start.8 = (bf16[1,512,256]{1,2,0:T(8,128)(2,1)S(1)}, bf16[1,512,256]{1,2,0:T(8,128)(2,1)}, u32[]{:S(2)}) copy-start(bf16[1,512,256]{1,2,0:T(8,128)(2,1)} %get-tuple-element.158) | copy-start | bytes 786436 | tf_op jit(solution)/shard_map/while/body/eval_jaxpr/cond
  88.0 5.2 %copy-start.1 = (bf16[1,512,256]{1,2,0:T(8,128)(2,1)S(1)}, bf16[1,512,256]{1,2,0:T(8,128)(2,1)}, u32[]{:S(2)}) copy-start(bf16[1,512,256]{1,2,0:T(8,128)(2,1)} %get-tuple-element.159) | copy-start | bytes 786436 | tf_op jit(solution)/shard_map/while/body/eval_jaxpr/cond
  97.6 42.6 %collective-permute-start.1 = (f32[2,512,256]{1,2,0:T(8,128)}, f32[2,512,256]{1,2,0:T(8,128)}, u32[]{:S(2)}, u32[]{:S(2)}) collective-permute-start(f32[2,512,256]{1,2,0:T(8,128)} %pad_maximum_fusion), channel_id=1, source_target_pairs={{0,1},{1,2},{2,3},{3,4},{4,5},{5,6},{6,7},{7,0},{8,9},{9,10},{10,1... | collective-permute-start | bytes 3145736 | tf_op jit(solution)/shard_map/while/body/eval_jaxpr/ppermute | solution.py:17
  97.6 20.0 %collective-permute-start = (bf16[2,512,256]{2,1,0:T(8,128)(2,1)}, bf16[2,512,256]{2,1,0:T(8,128)(2,1)S(1)}, u32[]{:S(2)}, u32[]{:S(2)}) collective-permute-start(bf16[2,512,256]{2,1,0:T(8,128)(2,1)} %pad_maximum_fusion.1), channel_id=1, source_target_pairs={{0,1},{1,2},{2,3},{3,4},{4,5},{5,6},{6,7},{8,9},{9,10},{10,11},{11... | collective-permute-start | bytes 1572872 | tf_op jit(solution)/shard_map/while/body/eval_jaxpr/ppermute | solution.py:12
  117.7 0.9 copy-start.6
  122.0 1.3 copy-start.4
  136.4 16.9 %all-to-all-start.6 = ((bf16[4,128,1024]{2,1,0:T(8,128)(2,1)}), bf16[4,128,1024]{2,1,0:T(8,128)(2,1)S(1)}, u32[]{:S(2)}, u32[]{:S(2)}) async-start(bf16[4,128,1024]{2,1,0:T(8,128)(2,1)} %bitcast.64), calls=%async_computation.6 | async-start | bytes 2097152 | tf_op jit(solution)/shard_map/all_to_all | solution.py:149
  141.7 6.8 %collective-permute-start.2 = (bf16[2,512,256]{1,2,0:T(8,128)(2,1)S(1)}, bf16[2,512,256]{1,2,0:T(8,128)(2,1)S(1)}, u32[]{:S(2)}, u32[]{:S(2)}) collective-permute-start(bf16[2,512,256]{1,2,0:T(8,128)(2,1)S(1)} %fusion.22), channel_id=1, source_target_pairs={{0,7},{1,0},{2,1},{3,2},{4,3},{5,4},{6,5},{7,6},{8,15},{9,8},{10,9... | collective-permute-start | bytes 1572872 | tf_op jit(solution)/shard_map/ppermute | solution.py:17
  153.3 8.8 %all-to-all-start.8 = ((bf16[4,128,256]{2,1,0:T(8,128)(2,1)}), bf16[4,128,256]{2,1,0:T(8,128)(2,1)S(1)}, u32[]{:S(2)}, u32[]{:S(2)}) async-start(bf16[4,128,256]{2,1,0:T(8,128)(2,1)} %bitcast.70), calls=%async_computation.8 | async-start | bytes 524288 | tf_op jit(solution)/shard_map/all_to_all | solution.py:155
  162.1 8.8 %all-to-all-start.7 = ((bf16[4,128,256]{2,1,0:T(8,128)(2,1)}), bf16[4,128,256]{2,1,0:T(8,128)(2,1)S(1)}, u32[]{:S(2)}, u32[]{:S(2)}) async-start(bf16[4,128,256]{2,1,0:T(8,128)(2,1)} %bitcast.67), calls=%async_computation.7 | async-start | bytes 524288 | tf_op jit(solution)/shard_map/all_to_all | solution.py:152
where the time goes:
time: 173 us; the launch traced here: 172 us
  waiting for transfers between devices  68.6 us (40%)
  starting transfers between devices  35.1 us (20%)
  local copies, waits for them, and re-layouts  32.7 us (19%)
  matrix products  22.8 us (13%)
  other arithmetic  11.7 us (7%)
    ppermute x1, waiting for transfers between devices, shifted(): return lax.ppermute(value, axis, pairs)  16.4 us
    unnamed x15, local copies, waits for them, and re-layouts  13.7 us
    all_to_all x1, waiting for transfers between devices, local(): lax.all_to_all(out_grad, 'head', split_axis=1, concat_axis=0, tiled=True)  11.8 us
    all_to_all x1, waiting for transfers between devices, local(): lax.all_to_all(attn_out, 'head', split_axis=1, concat_axis=0, tiled=True)  9.04 us
    all_to_all x1, waiting for transfers between devices, local(): lax.all_to_all(query_in, 'head', split_axis=1, concat_axis=0, tiled=True)  6.73 us
    ppermute x2, waiting for transfers between devices, shifted_2(): lax.ppermute(value, axis, [(i, (i + by) % count) for i in range(count)])  6.69 us
    another operation x8, local copies, waits for them, and re-layouts  6.4 us
    dot_general x2, matrix products, block_terms(): jnp.einsum('qgjd,kgd->gjqk', dout_heads, value_heads, preferred_element_t...  5.95 us
  transfers between devices with their start and end apart: 12, of which 11 were waited for; matrix products, arithmetic and copies ran while one was open for 25% of the time, Pallas kernels for 0%

commit v1 on v0

--- a/solution.py
+++ b/solution.py
@@ -84,7 +84,12 @@
         lax.all_to_all(key_in, "head", split_axis=1, concat_axis=0, tiled=True),
         lax.all_to_all(value_in, "head", split_axis=1, concat_axis=0, tiled=True),
         lax.all_to_all(attn_out, "head", split_axis=1, concat_axis=0, tiled=True),
-        lax.all_to_all(out_grad, "head", split_axis=1, concat_axis=0, tiled=True),
+        jnp.concatenate(
+            lax.all_to_all(
+                jnp.stack(jnp.split(out_grad, lax.axis_size("head"), axis=1)), "head", 0, 0
+            ),
+            axis=0,
+        ),
     )
     norm_rows = lax.all_to_all(log_norm, "head", split_axis=1, concat_axis=0, tiled=True)
     dout_rows, output_rows = (output_rows, dout_rows)

time: 173 us -> 176 us (1.017)
  waiting for transfers between devices: 68.6 us -> 73 us
  local copies, waits for them, and re-layouts: 32.7 us -> 30.8 us
    all_to_all x1, waiting for transfers between devices: 9.04 us -> 11.9 us  [local(): lax.all_to_all(attn_out, 'head', split_axis=1, concat_axis=0, tiled=True)]
    unnamed x15 -> x12, local copies, waits for them, and re-layouts: 13.7 us -> 11 us
    another operation x8 -> x11, local copies, waits for them, and re-layouts: 6.4 us -> 7.78 us  [the longest x4 4.99 us: block_terms(): dout_heads = dout_rows.reshape(r, kv_local, group, HEAD_DIM)]
  transfers between devices with their start and end apart: 12 -> 12, of which waited for: 11 -> 11; matrix products, arithmetic and copies ran while one was open for 25% -> 24% of each run, Pallas kernels for 0% -> 0%
where the time goes in v1:
time: 176 us; the launch traced here: 175 us
  waiting for transfers between devices  73 us (41%)
  starting transfers between devices  35.5 us (20%)
  local copies, waits for them, and re-layouts  30.8 us (18%)
  matrix products  23.5 us (13%)
  other arithmetic  11.4 us (6%)
    ppermute x1, waiting for transfers between devices, shifted(): return lax.ppermute(value, axis, pairs)  16.4 us
    all_to_all x1, waiting for transfers between devices, local(): lax.all_to_all(attn_out, 'head', split_axis=1, concat_axis=0, tiled=True)  11.9 us
    unnamed x12, local copies, waits for them, and re-layouts  11 us
    all_to_all x1, waiting for transfers between devices, local(): lax.all_to_all(jnp.stack(jnp.split(out_grad, lax.axis_size('head'), axis=...  10.3 us
    all_to_all x1, waiting for transfers between devices, local(): lax.all_to_all(query_in, 'head', split_axis=1, concat_axis=0, tiled=True)  8.38 us
    ppermute x2, waiting for transfers between devices, shifted_2(): lax.ppermute(value, axis, [(i, (i + by) % count) for i in range(count)])  6.69 us
    dot_general x2, matrix products, block_terms(): jnp.einsum('qgjd,kgd->gjqk', dout_heads, value_heads, preferred_element_t...  5.92 us
    dot_general x2, matrix products, block_terms(): jnp.einsum('gjqk,qgjd->kgd', weights_low, dout_heads, preferred_element_t...  5.32 us
  transfers between devices with their start and end apart: 12, of which 11 were waited for; matrix products, arithmetic and copies ran while one was open for 24% of the time, Pallas kernels for 0%

profile of v1, /device:TPU:8, one launch (start us, length us, event | category | flops | bytes accessed | tf_op | source)
XLA Modules:
  0.0 175.3 jit_solution(12880726252387524644)
XLA Ops:
  2.5 3.7 %all-to-all-start = ((bf16[128,4,256]{0,2,1:T(8,128)(2,1)}), bf16[128,4,256]{0,2,1:T(8,128)(2,1)S(1)}, u32[]{:S(2)}, u32[]{:S(2)}) async-start(bf16[128,4,256]{0,2,1:T(8,128)(2,1)} %bitcast.42), calls=%async_computation | async-start | bytes 524288 | tf_op jit(solution)/shard_map/all_to_all | solution.py:84
  8.0 3.6 %all-to-all-done = bf16[128,4,256]{0,2,1:T(8,128)(2,1)S(1)} async-done(((bf16[128,4,256]{0,2,1:T(8,128)(2,1)}), bf16[128,4,256]{0,2,1:T(8,128)(2,1)S(1)}, u32[]{:S(2)}, u32[]{:S(2)}) %all-to-all-start) | async-done | bytes 262176 | tf_op jit(solution)/shard_map/all_to_all | solution.py:84
  11.6 4.0 %all-to-all-start.1 = ((bf16[128,4,256]{0,2,1:T(8,128)(2,1)}), bf16[128,4,256]{0,2,1:T(8,128)(2,1)}, u32[]{:S(2)}, u32[]{:S(2)}) async-start(bf16[128,4,256]{0,2,1:T(8,128)(2,1)} %bitcast.45), calls=%async_computation.1 | async-start | bytes 524288 | tf_op jit(solution)/shard_map/all_to_all | solution.py:85
  17.9 3.2 %all-to-all-done.1 = bf16[128,4,256]{0,2,1:T(8,128)(2,1)} async-done(((bf16[128,4,256]{0,2,1:T(8,128)(2,1)}), bf16[128,4,256]{0,2,1:T(8,128)(2,1)}, u32[]{:S(2)}, u32[]{:S(2)}) %all-to-all-start.1) | async-done | bytes 262176 | tf_op jit(solution)/shard_map/all_to_all | solution.py:85
  21.1 3.5 %all-to-all-start.2 = ((bf16[128,4,1024]{0,2,1:T(8,128)(2,1)}), bf16[128,4,1024]{0,2,1:T(8,128)(2,1)S(1)}, u32[]{:S(2)}, u32[]{:S(2)}) async-start(bf16[128,4,1024]{0,2,1:T(8,128)(2,1)} %bitcast.48), calls=%async_computation.2 | async-start | bytes 2097152 | tf_op jit(solution)/shard_map/all_to_all | solution.py:83
  27.6 8.4 %all-to-all-done.2 = bf16[128,4,1024]{0,2,1:T(8,128)(2,1)S(1)} async-done(((bf16[128,4,1024]{0,2,1:T(8,128)(2,1)}), bf16[128,4,1024]{0,2,1:T(8,128)(2,1)S(1)}, u32[]{:S(2)}, u32[]{:S(2)}) %all-to-all-start.2) | async-done | bytes 1048608 | tf_op jit(solution)/shard_map/all_to_all | solution.py:83
  35.9 3.5 %all-to-all-start.5 = ((bf16[128,4,1024]{2,0,1:T(8,128)(2,1)}), bf16[128,4,1024]{2,0,1:T(8,128)(2,1)S(1)}, u32[]{:S(2)}, u32[]{:S(2)}) async-start(bf16[128,4,1024]{2,0,1:T(8,128)(2,1)} %copy.103), calls=%async_computation.5 | async-start | bytes 2097152 | tf_op jit(solution)/shard_map/all_to_all | solution.py:86
  40.7 11.9 %all-to-all-done.5 = bf16[128,4,1024]{2,0,1:T(8,128)(2,1)S(1)} async-done(((bf16[128,4,1024]{2,0,1:T(8,128)(2,1)}), bf16[128,4,1024]{2,0,1:T(8,128)(2,1)S(1)}, u32[]{:S(2)}, u32[]{:S(2)}) %all-to-all-start.5) | async-done | bytes 1048608 | tf_op jit(solution)/shard_map/all_to_all | solution.py:86
  52.6 3.5 %all-to-all-start.4 = ((bf16[4,128,1024]{2,1,0:T(8,128)(2,1)}), bf16[4,128,1024]{2,1,0:T(8,128)(2,1)S(1)}, u32[]{:S(2)}, u32[]{:S(2)}) async-start(bf16[4,128,1024]{2,1,0:T(8,128)(2,1)} %pad_maximum_fusion), calls=%async_computation.4 | async-start | bytes 2097152 | tf_op jit(solution)/shard_map/all_to_all | solution.py:88
  59.0 10.3 %all-to-all-done.4 = bf16[4,128,1024]{2,1,0:T(8,128)(2,1)S(1)} async-done(((bf16[4,128,1024]{2,1,0:T(8,128)(2,1)}), bf16[4,128,1024]{2,1,0:T(8,128)(2,1)S(1)}, u32[]{:S(2)}, u32[]{:S(2)}) %all-to-all-start.4) | async-done | bytes 1048608 | tf_op jit(solution)/shard_map/all_to_all | solution.py:88
  69.2 3.3 %all-to-all-start.3 = ((f32[128,4,8]{0,2,1:T(8,128)}), f32[128,4,8]{0,2,1:T(8,128)S(1)}, u32[]{:S(2)}, u32[]{:S(2)}) async-start(f32[128,4,8]{0,2,1:T(8,128)} %bitcast.51), calls=%async_computation.3 | async-start | bytes 32768 | tf_op jit(solution)/shard_map/all_to_all | solution.py:94
  77.2 19.3 %conditional.2 = (f32[512,1024]{0,1:T(8,128)}, f32[1,512,256]{1,2,0:T(8,128)}, f32[1,512,256]{1,2,0:T(8,128)}) conditional(s32[]{:T(128)} %convert_element_type.49, () %tuple.34, (s32[512]{0:T(512)S(1)}, s32[]{:T(128)}, s32[4096]{0:T(1024)}, s32[]{:T(128)}, bf16[2,512,256]{2,1,0:T(8,128)(2,1)}, /*index=5*/bf16[512,1024]{1,0:T(8,128)(2,1)S(1)}, ...), branch_computations={%region_1.2_spmd, %region_2.3_spmd} | conditional | flops 2706768896 | bytes 62554304 | solution.py:132
  86.5 2.7 %fusion.5 = f32[2,512,128,1]{1,2,3,0:T(8,128)} fusion(bf16[512,2,4,128]{0,3,2,1:T(8,128)(2,1)S(1)} %copy-done.3, f32[2,512,512,4]{2,1,3,0:T(8,128)S(1)} %fusion.26, f32[2,4,512]{2,1,0:T(4,128)S(1)} %bitcast.192, pred[512,512]{0,1:T(8,128)(4,1)S(1)} %copy-done.5), kind=kOutput, calls=%fused_computation.7 | convolution fusion | flops 545259520 | bytes 10240000 | tf_op jit(solution)/shard_map/while/body/eval_jaxpr/cond/branch_1_fun/gjqk,qgjd->kgd/dot_general | solution.py:53
  89.2 3.0 %fusion.1 = bf16[2,4,512,512]{2,3,1,0:T(8,128)(2,1)S(1)} fusion(f32[2,512,512,4]{2,1,3,0:T(8,128)S(1)} %fusion.26, f32[2,4,512]{2,1,0:T(4,128)S(1)} %bitcast.190, f32[2,4,512]{2,1,0:T(4,128)S(1)} %bitcast.193, pred[512,512]{0,1:T(8,128)(4,1)S(1)} %copy-done.5, bf16[512,2,128,1]{0,2,3,1:T(8,128)(2,1)S(1)} %bitcast.186, bf16[512,2,4,128]{0,3,2,1:T(8,128)(2,1)S(1)} %copy-done.3), kind=kOutput, calls=%fused_computation.2 | convolution fusion | flops 549453824 | bytes 14188544 | tf_op jit(solution)/shard_map/while/body/eval_jaxpr/cond/branch_1_fun/qgjd,kgd->gjqk/dot_general | solution.py:56
  98.8 3.6 %collective-permute-start = (bf16[2,512,256]{2,1,0:T(8,128)(2,1)}, bf16[2,512,256]{2,1,0:T(8,128)(2,1)S(1)}, u32[]{:S(2)}, u32[]{:S(2)}) collective-permute-start(bf16[2,512,256]{2,1,0:T(8,128)(2,1)} %pad_maximum_fusion.2), channel_id=1, source_target_pairs={{0,1},{1,2},{2,3},{3,4},{4,5},{5,6},{6,7},{8,9},{9,10},{10,11},{11... | collective-permute-start | bytes 1572872 | tf_op jit(solution)/shard_map/while/body/eval_jaxpr/ppermute | solution.py:12
  102.4 16.4 %collective-permute-done = bf16[2,512,256]{2,1,0:T(8,128)(2,1)S(1)} collective-permute-done((bf16[2,512,256]{2,1,0:T(8,128)(2,1)}, bf16[2,512,256]{2,1,0:T(8,128)(2,1)S(1)}, u32[]{:S(2)}, u32[]{:S(2)}) %collective-permute-start) | collective-permute-done | bytes 524320 | tf_op jit(solution)/shard_map/while/body/eval_jaxpr/ppermute | solution.py:12
  118.8 17.2 %conditional.3 = (f32[512,1024]{0,1:T(8,128)}, f32[1,512,256]{1,2,0:T(8,128)}, f32[1,512,256]{1,2,0:T(8,128)}) conditional(s32[]{:T(128)} %convert_element_type.53, () %tuple.36, (s32[512]{0:T(512)S(1)}, s32[]{:T(128)}, s32[4096]{0:T(1024)}, s32[]{:T(128)}, bf16[2,512,256]{2,1,0:T(8,128)(2,1)S(1)}, /*index=5*/bf16[512,1024]{1,0:T(8,128)(2,1)S(1)}, ...), branch_computations={%region_3.4_spmd, %region_4.5_spmd} | conditional | flops 2706768896 | bytes 61505704 | solution.py:132
  128.7 3.0 %fusion.12 = bf16[2,4,512,512]{2,3,1,0:T(8,128)(2,1)S(1)} fusion(f32[2,512,512,4]{2,1,3,0:T(8,128)S(1)} %fusion.27, f32[2,4,512]{2,1,0:T(4,128)S(1)} %bitcast.191, f32[2,4,512]{2,1,0:T(4,128)S(1)} %bitcast.195, pred[512,512]{0,1:T(8,128)(4,1)S(1)} %copy-done.6, bf16[512,2,128,1]{0,2,3,1:T(8,128)(2,1)S(1)} %bitcast.187, ...), kind=kOutput, calls=%fused_computation.19 | convolution fusion | flops 549453824 | bytes 14188544 | tf_op jit(solution)/shard_map/cond/branch_1_fun/qgjd,kgd->gjqk/dot_general | solution.py:56
  139.9 3.5 %all-to-all-start.6 = ((bf16[4,128,1024]{2,1,0:T(8,128)(2,1)}), bf16[4,128,1024]{2,1,0:T(8,128)(2,1)S(1)}, u32[]{:S(2)}, u32[]{:S(2)}) async-start(bf16[4,128,1024]{2,1,0:T(8,128)(2,1)} %bitcast.62), calls=%async_computation.6 | async-start | bytes 2097152 | tf_op jit(solution)/shard_map/all_to_all | solution.py:154
  145.2 6.7 %collective-permute-done.2 = bf16[2,512,256]{1,2,0:T(8,128)(2,1)S(1)} collective-permute-done((bf16[2,512,256]{1,2,0:T(8,128)(2,1)S(1)}, bf16[2,512,256]{1,2,0:T(8,128)(2,1)S(1)}, u32[]{:S(2)}, u32[]{:S(2)}) %collective-permute-start.2) | collective-permute-done | bytes 524320 | tf_op jit(solution)/shard_map/ppermute | solution.py:17
  152.8 4.0 %all-to-all-done.6 = bf16[4,128,1024]{2,1,0:T(8,128)(2,1)S(1)} async-done(((bf16[4,128,1024]{2,1,0:T(8,128)(2,1)}), bf16[4,128,1024]{2,1,0:T(8,128)(2,1)S(1)}, u32[]{:S(2)}, u32[]{:S(2)}) %all-to-all-start.6) | async-done | bytes 1048608 | tf_op jit(solution)/shard_map/all_to_all | solution.py:154
  156.8 3.4 %all-to-all-start.8 = ((bf16[4,128,256]{2,1,0:T(8,128)(2,1)}), bf16[4,128,256]{2,1,0:T(8,128)(2,1)S(1)}, u32[]{:S(2)}, u32[]{:S(2)}) async-start(bf16[4,128,256]{2,1,0:T(8,128)(2,1)} %bitcast.68), calls=%async_computation.8 | async-start | bytes 524288 | tf_op jit(solution)/shard_map/all_to_all | solution.py:160
  161.1 4.5 %all-to-all-done.8 = bf16[4,128,256]{2,1,0:T(8,128)(2,1)S(1)} async-done(((bf16[4,128,256]{2,1,0:T(8,128)(2,1)}), bf16[4,128,256]{2,1,0:T(8,128)(2,1)S(1)}, u32[]{:S(2)}, u32[]{:S(2)}) %all-to-all-start.8) | async-done | bytes 262176 | tf_op jit(solution)/shard_map/all_to_all | solution.py:160
  165.6 3.4 %all-to-all-start.7 = ((bf16[4,128,256]{2,1,0:T(8,128)(2,1)}), bf16[4,128,256]{2,1,0:T(8,128)(2,1)S(1)}, u32[]{:S(2)}, u32[]{:S(2)}) async-start(bf16[4,128,256]{2,1,0:T(8,128)(2,1)} %bitcast.65), calls=%async_computation.7 | async-start | bytes 524288 | tf_op jit(solution)/shard_map/all_to_all | solution.py:157
  (80 shorter events, 61.3 us)
Async XLA Ops:
  0.6 38.8 %copy-start.2 = (bf16[128,4096]{1,0:T(8,128)(2,1)S(1)}, bf16[128,4096]{1,0:T(8,128)(2,1)}, u32[]{:S(2)}) copy-start(bf16[128,4096]{1,0:T(8,128)(2,1)} %param.15) | copy-start | bytes 3145732
  2.5 9.1 %all-to-all-start = ((bf16[128,4,256]{0,2,1:T(8,128)(2,1)}), bf16[128,4,256]{0,2,1:T(8,128)(2,1)S(1)}, u32[]{:S(2)}, u32[]{:S(2)}) async-start(bf16[128,4,256]{0,2,1:T(8,128)(2,1)} %bitcast.42), calls=%async_computation | async-start | bytes 524288 | tf_op jit(solution)/shard_map/all_to_all | solution.py:84
  11.6 9.5 %all-to-all-start.1 = ((bf16[128,4,256]{0,2,1:T(8,128)(2,1)}), bf16[128,4,256]{0,2,1:T(8,128)(2,1)}, u32[]{:S(2)}, u32[]{:S(2)}) async-start(bf16[128,4,256]{0,2,1:T(8,128)(2,1)} %bitcast.45), calls=%async_computation.1 | async-start | bytes 524288 | tf_op jit(solution)/shard_map/all_to_all | solution.py:85
  21.1 14.8 %all-to-all-start.2 = ((bf16[128,4,1024]{0,2,1:T(8,128)(2,1)}), bf16[128,4,1024]{0,2,1:T(8,128)(2,1)S(1)}, u32[]{:S(2)}, u32[]{:S(2)}) async-start(bf16[128,4,1024]{0,2,1:T(8,128)(2,1)} %bitcast.48), calls=%async_computation.2 | async-start | bytes 2097152 | tf_op jit(solution)/shard_map/all_to_all | solution.py:83
  35.9 16.6 %copy-start = (bf16[128,4,1024]{0,2,1:T(8,128)(2,1)}, bf16[128,4,1024]{0,2,1:T(8,128)(2,1)S(1)}, u32[]{:S(2)}) copy-start(bf16[128,4,1024]{0,2,1:T(8,128)(2,1)S(1)} %all-to-all-done.2) | copy-start | bytes 3145732
  35.9 16.6 %all-to-all-start.5 = ((bf16[128,4,1024]{2,0,1:T(8,128)(2,1)}), bf16[128,4,1024]{2,0,1:T(8,128)(2,1)S(1)}, u32[]{:S(2)}, u32[]{:S(2)}) async-start(bf16[128,4,1024]{2,0,1:T(8,128)(2,1)} %copy.103), calls=%async_computation.5 | async-start | bytes 2097152 | tf_op jit(solution)/shard_map/all_to_all | solution.py:86
  52.6 16.6 %all-to-all-start.4 = ((bf16[4,128,1024]{2,1,0:T(8,128)(2,1)}), bf16[4,128,1024]{2,1,0:T(8,128)(2,1)S(1)}, u32[]{:S(2)}, u32[]{:S(2)}) async-start(bf16[4,128,1024]{2,1,0:T(8,128)(2,1)} %pad_maximum_fusion), calls=%async_computation.4 | async-start | bytes 2097152 | tf_op jit(solution)/shard_map/all_to_all | solution.py:88
  69.2 7.9 %all-to-all-start.3 = ((f32[128,4,8]{0,2,1:T(8,128)}), f32[128,4,8]{0,2,1:T(8,128)S(1)}, u32[]{:S(2)}, u32[]{:S(2)}) async-start(f32[128,4,8]{0,2,1:T(8,128)} %bitcast.51), calls=%async_computation.3 | async-start | bytes 32768 | tf_op jit(solution)/shard_map/all_to_all | solution.py:94
  84.1 2.4 %copy-start.3 = (bf16[512,2,4,128]{0,3,2,1:T(8,128)(2,1)S(1)}, bf16[512,2,4,128]{0,3,2,1:T(8,128)(2,1)}, u32[]{:S(2)}) copy-start(bf16[512,2,4,128]{0,3,2,1:T(8,128)(2,1)} %copy.124) | copy-start | bytes 3145732 | tf_op jit(solution)/shard_map/while/body/eval_jaxpr/cond
  84.1 2.4 %copy-start.5 = (pred[512,512]{0,1:T(8,128)(4,1)S(1)}, pred[512,512]{0,1:T(8,128)(4,1)}, u32[]{:S(2)}) copy-start(pred[512,512]{0,1:T(8,128)(4,1)} %compare_and_fusion) | copy-start | bytes 786436 | tf_op jit(solution)/shard_map/while/body/eval_jaxpr/cond
  86.5 2.7 %copy-start.7 = (bf16[1,512,256]{1,2,0:T(8,128)(2,1)S(1)}, bf16[1,512,256]{1,2,0:T(8,128)(2,1)}, u32[]{:S(2)}) copy-start(bf16[1,512,256]{1,2,0:T(8,128)(2,1)} %get-tuple-element.173) | copy-start | bytes 786436 | tf_op jit(solution)/shard_map/while/body/eval_jaxpr/cond
  89.2 5.2 %copy-start.1 = (bf16[1,512,256]{1,2,0:T(8,128)(2,1)S(1)}, bf16[1,512,256]{1,2,0:T(8,128)(2,1)}, u32[]{:S(2)}) copy-start(bf16[1,512,256]{1,2,0:T(8,128)(2,1)} %get-tuple-element.174) | copy-start | bytes 786436 | tf_op jit(solution)/shard_map/while/body/eval_jaxpr/cond
  98.8 44.6 %collective-permute-start.1 = (f32[2,512,256]{1,2,0:T(8,128)}, f32[2,512,256]{1,2,0:T(8,128)}, u32[]{:S(2)}, u32[]{:S(2)}) collective-permute-start(f32[2,512,256]{1,2,0:T(8,128)} %pad_maximum_fusion.1), channel_id=1, source_target_pairs={{0,1},{1,2},{2,3},{3,4},{4,5},{5,6},{6,7},{7,0},{8,9},{9,10},{10,1... | collective-permute-start | bytes 3145736 | tf_op jit(solution)/shard_map/while/body/eval_jaxpr/ppermute | solution.py:17
  98.8 20.0 %collective-permute-start = (bf16[2,512,256]{2,1,0:T(8,128)(2,1)}, bf16[2,512,256]{2,1,0:T(8,128)(2,1)S(1)}, u32[]{:S(2)}, u32[]{:S(2)}) collective-permute-start(bf16[2,512,256]{2,1,0:T(8,128)(2,1)} %pad_maximum_fusion.2), channel_id=1, source_target_pairs={{0,1},{1,2},{2,3},{3,4},{4,5},{5,6},{6,7},{8,9},{9,10},{10,11},{11... | collective-permute-start | bytes 1572872 | tf_op jit(solution)/shard_map/while/body/eval_jaxpr/ppermute | solution.py:12
  124.2 1.9 %copy-start.4 = (bf16[512,2,4,128]{0,3,2,1:T(8,128)(2,1)S(1)}, bf16[512,2,4,128]{0,3,2,1:T(8,128)(2,1)}, u32[]{:S(2)}) copy-start(bf16[512,2,4,128]{0,3,2,1:T(8,128)(2,1)} %copy.134) | copy-start | bytes 3145732 | tf_op jit(solution)/shard_map/cond
  124.7 1.3 copy-start.6
  126.0 2.7 %copy-start.8 = (bf16[1,512,256]{1,2,0:T(8,128)(2,1)S(1)}, bf16[1,512,256]{1,2,0:T(8,128)(2,1)}, u32[]{:S(2)}) copy-start(bf16[1,512,256]{1,2,0:T(8,128)(2,1)} %get-tuple-element.177) | copy-start | bytes 786436 | tf_op jit(solution)/shard_map/cond
  139.9 16.9 %all-to-all-start.6 = ((bf16[4,128,1024]{2,1,0:T(8,128)(2,1)}), bf16[4,128,1024]{2,1,0:T(8,128)(2,1)S(1)}, u32[]{:S(2)}, u32[]{:S(2)}) async-start(bf16[4,128,1024]{2,1,0:T(8,128)(2,1)} %bitcast.62), calls=%async_computation.6 | async-start | bytes 2097152 | tf_op jit(solution)/shard_map/all_to_all | solution.py:154
  145.1 6.8 %collective-permute-start.2 = (bf16[2,512,256]{1,2,0:T(8,128)(2,1)S(1)}, bf16[2,512,256]{1,2,0:T(8,128)(2,1)S(1)}, u32[]{:S(2)}, u32[]{:S(2)}) collective-permute-start(bf16[2,512,256]{1,2,0:T(8,128)(2,1)S(1)} %fusion.22), channel_id=1, source_target_pairs={{0,7},{1,0},{2,1},{3,2},{4,3},{5,4},{6,5},{7,6},{8,15},{9,8},{10,9... | collective-permute-start | bytes 1572872 | tf_op jit(solution)/shard_map/ppermute | solution.py:17
  156.8 8.8 %all-to-all-start.8 = ((bf16[4,128,256]{2,1,0:T(8,128)(2,1)}), bf16[4,128,256]{2,1,0:T(8,128)(2,1)S(1)}, u32[]{:S(2)}, u32[]{:S(2)}) async-start(bf16[4,128,256]{2,1,0:T(8,128)(2,1)} %bitcast.68), calls=%async_computation.8 | async-start | bytes 524288 | tf_op jit(solution)/shard_map/all_to_all | solution.py:160
  165.6 8.8 %all-to-all-start.7 = ((bf16[4,128,256]{2,1,0:T(8,128)(2,1)}), bf16[4,128,256]{2,1,0:T(8,128)(2,1)S(1)}, u32[]{:S(2)}, u32[]{:S(2)}) async-start(bf16[4,128,256]{2,1,0:T(8,128)(2,1)} %bitcast.65), calls=%async_computation.7 | async-start | bytes 524288 | tf_op jit(solution)/shard_map/all_to_all | solution.py:157
